TPU v7x, 128 devices: a whole 4x4x4 slice. The times are simulated.
128 devices in a mesh: walk: 8 (over x, z_lo), pair: 16 (over y, z_hi, core).
Axes of the slice: x: 4, y: 4, z: 4 (z_hi: 2, z_lo: 2; z = z_hi * 2 + z_lo), core: 2. Of those that a mesh axis runs over, the one named last changes fastest.
Arguments:
- walkers: float32 [256, 64, 512], P(('walk', 'pair')), may hold values from -6 to 6
- inverse_intersection: float32 [256, 64, 64], P(('walk', 'pair')), may hold values from -0.75 to 0.75
- trial: bfloat16 [64, 512], P(None, 'walk'), may hold values from -0.095703125 to 0.095703125
- fields: float32 [256, 4096], P(('walk', 'pair')), may hold values from -6 to 6
- cholesky: bfloat16 [512, 512, 4096], P('pair', 'walk'), may hold values from -0.083984375 to 0.083984375
Outputs:
- advanced_walkers: float32 [256, 64, 512], P(('walk', 'pair'))
- log_importance: float32 [256], P(('walk', 'pair'))
All inputs are finite; a program needn't handle non-finite values.
Results may differ from a plain program's by a relative error of at most 0.011.
Values may be sent and summed in bfloat16 or wider, within the bound.
A program may use at most 128 MiB of HBM per device.

v0:
```python
import jax
import jax.numpy as jnp
from jax import lax
from jax.sharding import PartitionSpec as P

time_root = 0.1


def per_device(walkers, inverse_intersection, trial, fields, cholesky):
    highest = lax.Precision.HIGHEST
    pair_count = lax.axis_size("pair")
    walk_count = lax.axis_size("walk")
    local_walkers, occupied, orbitals = walkers.shape
    block_rows = cholesky.shape[0]
    block_cols = cholesky.shape[1]
    vectors = cholesky.shape[2]
    flat_slab = cholesky.reshape(block_rows * block_cols, vectors)
    split_walkers = walkers.reshape(local_walkers, occupied, pair_count, block_rows)
    rotated = jnp.einsum("wji,wjbr->wbir", inverse_intersection, split_walkers, precision=highest)
    rotated = rotated.astype(jnp.bfloat16).reshape(local_walkers, pair_count, occupied * block_rows)
    regrouped = lax.all_to_all(rotated, "pair", split_axis=1, concat_axis=0, tiled=True)
    shard_piece = lax.all_gather(regrouped, "walk", axis=0, tiled=True)
    rows_here = shard_piece.shape[0]
    rotated_piece = shard_piece.reshape(rows_here, occupied, block_rows)
    greens = jnp.einsum("wir,iq->wrq", rotated_piece, trial, preferred_element_type=jnp.float32)
    greens = greens.astype(jnp.bfloat16).reshape(rows_here, block_rows * block_cols)
    partial_bias = jnp.dot(greens, flat_slab, preferred_element_type=jnp.float32)
    force_bias = lax.psum_scatter(partial_bias, ("walk", "pair"), scatter_dimension=0, tiled=True)
    bias_shift = -time_root * force_bias
    log_importance = jnp.sum(fields * bias_shift - 0.5 * bias_shift * bias_shift, axis=1)
    own_shifted = (fields - bias_shift).astype(jnp.bfloat16)
    shifted = lax.all_gather(own_shifted, ("walk", "pair"), axis=0, tiled=True)
    potential = lax.dot_general(
        shifted, flat_slab, (((1,), (1,)), ((), ())), preferred_element_type=jnp.float32
    )
    potential = potential.astype(jnp.bfloat16)
    blocks = potential.reshape(walk_count * pair_count, local_walkers, block_rows, block_cols)
    arrived = lax.all_to_all(blocks, ("walk", "pair"), split_axis=0, concat_axis=0, tiled=True)
    arrived = arrived.reshape(walk_count, pair_count, local_walkers, block_rows, block_cols)
    series_term = walkers
    summed = walkers
    for degree in range(1, 7):
        operand = series_term.astype(jnp.bfloat16).reshape(
            local_walkers, occupied, walk_count, block_cols
        )
        product = jnp.einsum(
            "kiac,abkrc->kibr", operand, arrived, preferred_element_type=jnp.float32
        )
        series_term = product.reshape(local_walkers, occupied, orbitals) * (-time_root / degree)
        summed = summed + series_term
    return (summed, log_importance)


def solution(mesh):
    in_specs = (
        P(("walk", "pair"), None, None),
        P(("walk", "pair"), None, None),
        P(None, "walk"),
        P(("walk", "pair"), None),
        P("pair", "walk", None),
    )
    out_specs = (P(("walk", "pair"), None, None), P(("walk", "pair")))
    return jax.shard_map(
        per_device, mesh=mesh, in_specs=in_specs, out_specs=out_specs, check_vma=False
    )
```

profile of v0, /device:TPU:1, one launch (start us, length us, event | category | flops | bytes accessed | tf_op | source)
XLA Modules:
  0.0 483.9 jit_solution(9283367136357233023)
XLA Ops:
  7.2 0.0 all-gather.4.cloned.1.call-start
  7.2 1.1 copy.71
  8.4 0.6 fusion.5
  9.0 0.3 copy.98
  9.3 0.5 reshape.93
  9.8 16.8 %all_to_all.23 = bf16[2,16,2048]{2,0,1:T(2,128)(2,1)S(1)} all-to-all(bf16[2,16,2048]{2,0,1:T(2,128)(2,1)S(1)} %reshape.93), channel_id=1, replica_groups=mesh['walk'=8,'pair'=16] {'pair'}, dimensions={1} | all-to-all | bytes 262144 | tf_op jit(solution)/shard_map/all_to_all | solution.py:21
  26.6 0.7 all_to_all.19
  27.3 0.0 all-reduce.3.cloned.1.call-start
  27.3 31.9 %all-gather.4.cloned.1.call-done = bf16[256,1,2048]{2,0,1:T(8,128)(2,1)} async-done(((bf16[32,1,2048]{2,0,1:T(8,128)(2,1)}), bf16[256,1,2048]{2,0,1:T(8,128)(2,1)}) %all-gather.4.cloned.1.call-update) | async-done | bytes 1048592 | tf_op jit(solution)/shard_map/all_gather | solution.py:22
  59.2 1.5 copy.66
  60.7 11.0 %convolution_bitcast_fusion = f32[256,4096]{1,0:T(8,128)} fusion(bf16[32,64,4096]{2,1,0:T(8,128)(2,1)} %param.9, bf16[256,64,32]{0,2,1:T(8,128)(2,1)S(1)} %bitcast.126, bf16[64,64]{1,0:T(8,128)(2,1)S(1)} %copy-done.3), kind=kOutput, calls=%fused_computation | convolution fusion | flops 4362600448 | bytes 22028288 | tf_op jit(solution)/shard_map/dot_general | solution.py:27
  71.7 0.0 all-gather.6.cloned.1.call-start
  71.8 158.5 %all-reduce.3.cloned.1.call-done = f32[256,4096]{1,0:T(8,128)} async-done(((f32[256,4096]{1,0:T(8,128)}), f32[256,4096]{1,0:T(8,128)}) %all-reduce.3.cloned.1.call-update) | async-done | bytes 4194320
  230.3 2.2 subtract_reduce_fusion
  232.5 192.5 %all-gather.6.cloned.1.call-done = bf16[128,2,4096]{2,1,0:T(2,128)(2,1)} async-done(((bf16[1,2,4096]{2,1,0:T(2,128)(2,1)}), bf16[128,2,4096]{2,1,0:T(2,128)(2,1)}) %all-gather.6.cloned.1.call-update) | async-done | bytes 2097168 | tf_op jit(solution)/shard_map/all_gather | solution.py:32
  424.9 2.7 reshape.77
  427.7 9.2 %convolution_convert_fusion = bf16[256,2048]{1,0:T(8,128)(2,1)} fusion(bf16[256,4096]{1,0:T(8,128)(2,1)S(1)} %reshape.77, bf16[2048,4096]{1,0:T(8,128)(2,1)} %bitcast.130), kind=kOutput, calls=%fused_computation.1 | convolution fusion | flops 4295491584 | bytes 19922944 | tf_op jit(solution)/shard_map/dot_general | solution.py:33
  436.9 3.3 reshape.73
  440.3 2.3 reshape.94
  442.6 7.5 %all-to-all-start.1 = ((bf16[128,2,2048]{2,1,0:T(2,128)(2,1)}), bf16[128,2,2048]{2,1,0:T(2,128)(2,1)}, u32[]{:S(2)}, u32[]{:S(2)}) async-start(bf16[128,2,2048]{2,1,0:T(2,128)(2,1)} %reshape.94), calls=%async_computation.1 | async-start | bytes 2097152 | tf_op jit(solution)/shard_map/all_to_all | solution.py:38
  450.2 0.2 reshape.75
  450.4 18.3 %all-to-all-done.1 = bf16[128,2,2048]{2,1,0:T(2,128)(2,1)} async-done(((bf16[128,2,2048]{2,1,0:T(2,128)(2,1)}), bf16[128,2,2048]{2,1,0:T(2,128)(2,1)}, u32[]{:S(2)}, u32[]{:S(2)}) %all-to-all-start.1) | async-done | bytes 1048608 | tf_op jit(solution)/shard_map/all_to_all | solution.py:38
  468.7 3.8 reshape.95
  472.5 0.7 fusion.18
  473.2 0.1 fusion.25
  473.3 0.6 fusion.26
  473.9 0.6 fusion.27
  474.5 0.6 fusion.28
  475.1 0.6 fusion.29
  475.7 0.6 fusion
  476.3 0.2 fusion.17
  476.5 0.9 copy.82
  (12 shorter events, 0.1 us)
Async XLA Ops:
  7.2 1.2 copy-start
  7.2 52.0 %all-gather.4.cloned.1.call-start = ((), (), s32[]{:S(2)}) async-start(), calls=%async_computation.2 | async-start | bytes 1179648 | tf_op jit(solution)/shard_map/all_gather | solution.py:22
  9.0 51.7 %copy-start.3 = (bf16[64,64]{1,0:T(8,128)(2,1)S(1)}, bf16[64,64]{1,0:T(8,128)(2,1)}, u32[]{:S(2)}) copy-start(bf16[64,64]{1,0:T(8,128)(2,1)} %param.7) | copy-start | bytes 24580
  27.3 203.0 %all-reduce.3.cloned.1.call-start = ((), (), s32[]{:S(2)}) async-start(), calls=%async_computation.4 | async-start | bytes 8388608
  71.7 158.6 %copy-start.2 = (f32[2,4096]{1,0:T(2,128)S(1)}, f32[2,4096]{1,0:T(2,128)}, u32[]{:S(2)}) copy-start(f32[2,4096]{1,0:T(2,128)} %param.8) | copy-start | bytes 98308
  71.7 353.2 %all-gather.6.cloned.1.call-start = ((), (), s32[]{:S(2)}) async-start(), calls=%async_computation.3 | async-start | bytes 2113536 | tf_op jit(solution)/shard_map/all_gather | solution.py:32
  440.3 9.9 %copy-start.1 = (f32[2,64,512]{2,1,0:T(8,128)S(1)}, f32[2,64,512]{2,1,0:T(8,128)}, u32[]{:S(2)}) copy-start(f32[2,64,512]{2,1,0:T(8,128)} %param.5) | copy-start | bytes 786436
  442.6 26.1 %all-to-all-start.1 = ((bf16[128,2,2048]{2,1,0:T(2,128)(2,1)}), bf16[128,2,2048]{2,1,0:T(2,128)(2,1)}, u32[]{:S(2)}, u32[]{:S(2)}) async-start(bf16[128,2,2048]{2,1,0:T(2,128)(2,1)} %reshape.94), calls=%async_computation.1 | async-start | bytes 2097152 | tf_op jit(solution)/shard_map/all_to_all | solution.py:38
Sparse Core Ops, SparseCore 0:
  27.4 31.7 all-gather.3
  71.9 158.3 all-reduce.2
  232.6 192.3 all-gather.5
where the time goes:
time: 484 us
  waiting for transfers between devices  401 us (83%)
  matrix products  24.5 us (5%)
  local copies, waits for them, and re-layouts  17.4 us (4%)
  blocking collectives  16.8 us (3%)
  between operations  13.9 us (3%)
  starting transfers between devices  7.66 us (2%)
    all_gather x1, waiting for transfers between devices, per_device(): shifted = lax.all_gather(own_shifted, ('walk', 'pair'), axis=0, tiled=True)  192 us
    unnamed x4, waiting for transfers between devices  159 us
    all_gather x1, waiting for transfers between devices, per_device(): shard_piece = lax.all_gather(regrouped, 'walk', axis=0, tiled=True)  31.9 us
    all_to_all x1, waiting for transfers between devices, per_device(): lax.all_to_all(blocks, ('walk', 'pair'), split_axis=0, concat_axis=0, til...  18.3 us
    all_to_all x1, blocking collectives, per_device(): lax.all_to_all(rotated, 'pair', split_axis=1, concat_axis=0, tiled=True)  16.8 us
    dot_general x1, matrix products, per_device(): jnp.dot(greens, flat_slab, preferred_element_type=jnp.float32)  11 us
    unnamed x13, local copies, waits for them, and re-layouts  10.9 us
  transfers between devices with their start and end apart: 4, of which 4 were waited for; matrix products, arithmetic and copies ran while one was open for 0% of the time, Pallas kernels for 0%

commit v1 on v0

v1 whole, which is shorter than its diff:
```python
import functools

import jax
import jax.numpy as jnp
from jax import lax
from jax.experimental import pallas as pl
from jax.experimental.pallas import tpu as pltpu
from jax.sharding import PartitionSpec as P

MESH = pl.DeviceIdType.MESH
F32 = jnp.float32
BF16 = jnp.bfloat16
time_root = 0.1
CHUNKS = 4
FIRST_AXIS = ("x", "y", "z", "x")
REST = {"x": (4, 2, 2), "y": (2, 4, 2), "z": (4, 4)}


def device_of(pos):
    x, y, zh, zl, c = pos
    return (x * 2 + zl, (y * 2 + zh) * 2 + c)


def moved(pos, axis, d):
    x, y, zh, zl, c = pos
    if axis == "x":
        return (lax.rem(x + d, 4), y, zh, zl, c)
    if axis == "y":
        return (x, lax.rem(y + d, 4), zh, zl, c)
    z = lax.rem(zh * 2 + zl + d, 4)
    return (x, y, z // 2, lax.rem(z, 2), c)


def slab_index(axis, pos):
    x, y, zh, zl, _ = pos
    every = slice(None)
    return {"x": (every, every, x), "y": (y,), "z": (every, zh, every, zl)}[axis]


def tile_index(axis, pos):
    x, y, zh, zl, _ = pos
    return {"x": (y, zh, zl), "y": (zh, x, zl), "z": (y, x)}[axis]


def kernel(
    walkers, inverse, trial, fields, cholesky, out, log_out,
    slab, half, diag, send_a, recv_a, wide, left, fields_out, fields_in,
    parts, from_core, sums, shifted, total, send_d, recv_d, potential, logs, logs_in,
    *rest,
):
    first_in = rest[:CHUNKS]
    first_sum = rest[CHUNKS : 2 * CHUNKS]
    slab_sem, send_sem, recv_sem, hop_send, hop_recv = rest[2 * CHUNKS :]
    a, b = lax.axis_index("walk"), lax.axis_index("pair")
    x, zl = a // 2, lax.rem(a, 2)
    c = lax.rem(b, 2)
    y, zh = b // 4, lax.rem(b // 2, 2)
    here = (x, y, zh, zl, c)
    slot = c * 64 + (b // 2) * 8 + a

    def other(i):
        dx, dy, dz, dc = lax.rem(i // 2, 4), lax.rem(i // 8, 4), i // 32, lax.rem(i, 2)
        px, py, pzh, pzl, _ = moved(moved(moved(here, "x", dx), "y", dy), "z", dz)
        return (px, py, pzh, pzl, lax.rem(c + dc, 2))

    def send(src, dst, sems, pos):
        pltpu.make_async_remote_copy(
            src_ref=src, dst_ref=dst, send_sem=sems[0], recv_sem=sems[1],
            device_id=device_of(pos), device_id_type=MESH,
        ).start()

    def wait(ref, sem):
        pltpu.make_async_copy(ref, ref, sem).wait()

    for r in range(32):
        place = (r % 16) * 2 + r // 16
        pltpu.make_async_copy(
            cholesky.at[r], slab.at[pl.ds(place * 64, 64)], slab_sem.at[place // 4]
        ).start()

    barrier = pltpu.get_barrier_semaphore()

    def greet(i, carry):
        pl.semaphore_signal(barrier, inc=1, device_id=device_of(other(i)), device_id_type=MESH)
        return carry

    lax.fori_loop(1, 128, greet, 0)

    for k in range(2):
        turned = jnp.transpose(walkers[k])
        rotated = jnp.dot(
            turned, inverse[k], precision=lax.Precision.HIGHEST, preferred_element_type=F32
        )
        rotated = rotated.reshape(16, 2, 16, 64)
        send_a[:, k] = jnp.concatenate([rotated[:, 0], rotated[:, 1]], axis=-1).astype(BF16)
        for n in range(CHUNKS):
            for to in range(8):
                row = fields[pl.ds(k, 1), pl.ds((n * 8 + to) * 128, 128)]
                fields_out[to, pl.ds(k * 4 + n, 1), :] = row

    pl.semaphore_wait(barrier, 127)

    def send_rotated(i, carry):
        pos = other(i)
        to = device_of(pos)
        send(send_a.at[to[1]], recv_a.at[slot], (send_sem.at[0], recv_sem.at[0]), pos)
        return carry

    lax.fori_loop(1, 128, send_rotated, 0)
    recv_a[slot] = send_a[b]

    def walk_peer(i):
        return (lax.rem(x + i // 2, 4), y, zh, lax.rem(zl + i, 2), c)

    def send_fields(i, carry):
        pos = walk_peer(i)
        to = device_of(pos)
        send(
            fields_out.at[to[0]], fields_in.at[pl.ds(pl.multiple_of(a * 8, 8), 8)],
            (send_sem.at[1], recv_sem.at[1]), pos,
        )
        return carry

    lax.fori_loop(1, 8, send_fields, 0)
    fields_in[pl.ds(pl.multiple_of(a * 8, 8), 8)] = fields_out[a]

    square = jnp.concatenate([trial[...].astype(F32)] * 4, axis=0)
    square = jnp.concatenate([square] * 4, axis=1)
    rows = lax.broadcasted_iota(jnp.int32, (256, 256), 0) // 64
    cols = lax.broadcasted_iota(jnp.int32, (256, 256), 1) // 64
    diag[...] = jnp.where(rows == cols, square, 0.0).astype(BF16)

    def rotate_group(g, carry):
        block = pl.ds(pl.multiple_of(g * 256, 256), 256)
        wait(slab.at[block], slab_sem.at[g])

        def columns(t, carry):
            lanes = pl.ds(pl.multiple_of(t * 256, 256), 256)
            half[block, lanes] = jnp.dot(
                diag[...], slab[block, lanes], preferred_element_type=F32
            ).astype(BF16)
            return carry

        return lax.fori_loop(0, 16, columns, carry)

    lax.fori_loop(0, 8, rotate_group, 0)

    wait(recv_a.at[pl.ds(0, 127)], recv_sem.at[0])

    def regroup(g, carry):
        base = pl.multiple_of(g * 256, 256)
        wide[pl.ds(base, 256), :] = recv_a[pl.ds(g * 8, 8)].astype(F32).reshape(256, 128)
        for j in range(16):
            left[pl.ds(pl.multiple_of(g * 16, 16), 16), pl.ds(j * 128, 128)] = wide[
                pl.ds(base + j, 16, stride=16), :
            ].astype(BF16)
        return carry

    lax.fori_loop(0, 16, regroup, 0)

    def hop(n, stage):
        return hop_send.at[n * 6 + stage], hop_recv.at[n * 6 + stage]

    def bias_chunk(n):
        def columns(t, carry):
            lanes = pl.ds(pl.multiple_of(n * 1024 + t * 256, 256), 256)
            got = jnp.dot(left[...], half[:, lanes], preferred_element_type=F32).astype(BF16)
            for group in range(16):
                for lane in range(2):
                    parts[n, group // 8, (group // 2) % 4, group % 2, t, lane] = got[
                        group * 16 : group * 16 + 16, lane * 128 : lane * 128 + 128
                    ]
            return carry

        lax.fori_loop(0, 4, columns, 0)
        send(parts.at[n, 1 - c], from_core.at[n], hop(n, 0), (x, y, zh, zl, 1 - c))

    def add_core(n):
        wait(from_core.at[n], hop_recv.at[n * 6])

        def add(i, carry):
            both = parts[n, c, i].astype(F32) + from_core[n, i].astype(F32)
            parts[n, c, i] = both.astype(BF16)
            return carry

        lax.fori_loop(0, 4, add, 0)
        axis = FIRST_AXIS[n]
        for d in range(1, 4):
            pos = moved(here, axis, d)
            src = parts.at[(n, c) + slab_index(axis, pos)]
            send(src, first_in[n].at[d - 1], hop(n, 1), pos)

    def plane_peer(axis, i):
        one, two = {"x": ("y", "z"), "y": ("z", "x"), "z": ("x", "y")}[axis]
        return moved(moved(here, one, i // 4), two, lax.rem(i, 4))

    def add_first(n):
        axis = FIRST_AXIS[n]
        wait(first_in[n], hop_recv.at[n * 6 + 1])
        got = parts[(n, c) + slab_index(axis, here)].astype(F32)
        for d in range(3):
            got = got + first_in[n][d].astype(F32)
        first_sum[n][...] = got.astype(BF16)

        def give(i, carry):
            pos = plane_peer(axis, i)
            send(first_sum[n].at[tile_index(axis, pos)], sums.at[n, i - 1], hop(n, 2), pos)
            return carry

        lax.fori_loop(1, 16, give, 0)

    def shift(n):
        axis = FIRST_AXIS[n]
        if n == 0:
            wait(fields_in.at[pl.ds(0, 56)], recv_sem.at[1])
        wait(sums.at[n], hop_recv.at[n * 6 + 2])
        bias = first_sum[n][tile_index(axis, here)].astype(F32)
        for i in range(15):
            bias = bias + sums[n, i].astype(F32)
        bias_shift = -time_root * bias
        field = fields_in[pl.ds(n, 16, stride=4), :]
        term = field * bias_shift - 0.5 * bias_shift * bias_shift
        logs[...] = term if n == 0 else logs[...] + term
        place = (n, c, y, zh, x, zl)
        shifted[place] = (field - bias_shift).astype(BF16)

        def give(i, carry):
            send(shifted.at[place], shifted.at[place], hop(n, 3), plane_peer(axis, i))
            return carry

        lax.fori_loop(1, 16, give, 0)
        if n == CHUNKS - 1:
            logs_in[a] = logs[...]

            def give_logs(i, carry):
                sems = send_sem.at[2], recv_sem.at[2]
                send(logs, logs_in.at[a], sems, walk_peer(i))
                return carry

            lax.fori_loop(1, 8, give_logs, 0)

    def spread_plane(n):
        axis = FIRST_AXIS[n]
        wait(sums.at[n], hop_recv.at[n * 6 + 3])
        part = shifted.at[(n, c) + slab_index(axis, here)]
        for d in range(1, 4):
            send(part, part, hop(n, 4), moved(here, axis, d))

    def spread_core(n):
        wait(first_in[n], hop_recv.at[n * 6 + 4])
        part = shifted.at[n, c]
        send(part, part, hop(n, 5), (x, y, zh, zl, 1 - c))

    def potential_chunk(n):
        wait(shifted.at[n, 1 - c], hop_recv.at[n * 6 + 5])

        def columns(t, carry):
            block = pl.ds(pl.multiple_of(t * 256, 256), 256)
            got = jnp.zeros((256, 256), F32) if n == 0 else total[t]
            for i in range(4):
                both = [shifted[n, :, :, :, i, lane].reshape(256, 128) for lane in range(2)]
                got = got + lax.dot_general(
                    jnp.concatenate(both, axis=1),
                    slab[block, pl.ds(n * 1024 + i * 256, 256)],
                    (((1,), (1,)), ((), ())), preferred_element_type=F32,
                )
            if n < CHUNKS - 1:
                total[t] = got
            else:
                for lane in range(2):
                    wide[pl.ds(t * 2 + lane, 256, stride=16), :] = got[
                        :, lane * 128 : lane * 128 + 128
                    ]
            return carry

        lax.fori_loop(0, 8, columns, 0)

    steps = (bias_chunk, add_core, add_first, shift, spread_plane, spread_core, potential_chunk)
    for time in range(len(steps) + CHUNKS - 1):
        for n in range(CHUNKS):
            if 0 <= time - n < len(steps):
                steps[time - n](n)

    def narrow(g, carry):
        block = wide[pl.ds(pl.multiple_of(g * 256, 256), 256), :]
        send_d[pl.ds(g * 8, 8)] = block.astype(BF16).reshape(8, 2, 16, 128)
        return carry

    lax.fori_loop(0, 16, narrow, 0)

    def send_potential(i, carry):
        pos = other(i)
        px, py, pzh, pzl, pc = pos
        to = pc * 64 + (py * 2 + pzh) * 8 + px * 2 + pzl
        send(send_d.at[to], recv_d.at[b, a], (send_sem.at[3], recv_sem.at[3]), pos)
        return carry

    lax.fori_loop(1, 128, send_potential, 0)
    recv_d[b, a] = send_d[slot]

    wait(logs_in.at[pl.ds(0, 7)], recv_sem.at[2])
    all_logs = logs_in[0]
    for i in range(1, 8):
        all_logs = all_logs + logs_in[i]
    log_rows = lax.broadcasted_iota(jnp.int32, (16, 128), 0)
    for k in range(2):
        log_out[k] = jnp.sum(jnp.where(log_rows == a * 2 + k, all_logs, 0.0))

    wait(recv_a.at[pl.ds(0, 127)], recv_sem.at[3])

    def assemble(i, carry):
        for k in range(2):
            for h in range(2):
                for pair in range(4):
                    both = [
                        recv_d[i, pair * 2 + e, k].astype(F32)[:, h * 64 : h * 64 + 64]
                        for e in range(2)
                    ]
                    potential[
                        k, pl.ds(pl.multiple_of(i * 32 + h * 16, 16), 16),
                        pl.ds(pair * 128, 128),
                    ] = jnp.concatenate(both, axis=1).astype(BF16)
        return carry

    lax.fori_loop(0, 16, assemble, 0)

    terms = [walkers[k] for k in range(2)]
    results = list(terms)
    for degree in range(1, 7):
        for k in range(2):
            product = lax.dot_general(
                terms[k].astype(BF16), potential[k], (((1,), (1,)), ((), ())),
                preferred_element_type=F32,
            )
            terms[k] = product * (-time_root / degree)
            results[k] = results[k] + terms[k]
    for k in range(2):
        out[k] = results[k]

    wait(recv_a.at[pl.ds(0, 127)], send_sem.at[0])
    wait(fields_in.at[pl.ds(0, 56)], send_sem.at[1])
    wait(logs_in.at[pl.ds(0, 7)], send_sem.at[2])
    wait(recv_a.at[pl.ds(0, 127)], send_sem.at[3])
    for n in range(CHUNKS):
        for stage, size in enumerate(
            (from_core.at[n], first_in[n], sums.at[n], sums.at[n], first_in[n], from_core.at[n])
        ):
            wait(size, hop_send.at[n * 6 + stage])


def per_device(walkers, inverse_intersection, trial, fields, cholesky):
    vmem = pl.BlockSpec(memory_space=pltpu.VMEM)
    tile = (16, 128)
    chunk = (4, 2, 4, 2) + tile
    scratch = [
        pltpu.VMEM((2048, 4096), BF16),
        pltpu.VMEM((2048, 4096), BF16),
        pltpu.VMEM((256, 256), BF16),
        pltpu.VMEM((16, 2) + tile, BF16),
        pltpu.VMEM((128, 2) + tile, BF16),
        pltpu.VMEM((4096, 128), F32),
        pltpu.VMEM((256, 2048), BF16),
        pltpu.VMEM((8, 8, 128), F32),
        pltpu.VMEM((64, 128), F32),
        pltpu.VMEM((CHUNKS, 2) + chunk, BF16),
        pltpu.VMEM((CHUNKS,) + chunk, BF16),
        pltpu.VMEM((CHUNKS, 15) + tile, BF16),
        pltpu.VMEM((CHUNKS, 2) + chunk, BF16),
        pltpu.VMEM((8, 256, 256), F32),
        pltpu.VMEM((128, 2) + tile, BF16),
        pltpu.VMEM((16, 8, 2) + tile, BF16),
        pltpu.VMEM((2, 512, 512), BF16),
        pltpu.VMEM(tile, F32),
        pltpu.VMEM((8,) + tile, F32),
        *[pltpu.VMEM((3,) + REST[axis] + tile, BF16) for axis in FIRST_AXIS],
        *[pltpu.VMEM(REST[axis] + tile, BF16) for axis in FIRST_AXIS],
        pltpu.SemaphoreType.DMA((8,)),
        pltpu.SemaphoreType.DMA((4,)),
        pltpu.SemaphoreType.DMA((4,)),
        pltpu.SemaphoreType.DMA((CHUNKS * 6,)),
        pltpu.SemaphoreType.DMA((CHUNKS * 6,)),
    ]
    advanced, log_importance = pl.pallas_call(
        kernel,
        out_shape=(
            jax.ShapeDtypeStruct(walkers.shape, F32),
            jax.ShapeDtypeStruct((2,), F32),
        ),
        in_specs=[vmem, vmem, vmem, vmem, pl.BlockSpec(memory_space=pl.ANY)],
        out_specs=(vmem, pl.BlockSpec(memory_space=pltpu.SMEM)),
        scratch_shapes=scratch,
        compiler_params=pltpu.CompilerParams(
            collective_id=0, has_side_effects=True, vmem_limit_bytes=62 * 1024 * 1024
        ),
    )(walkers, inverse_intersection, trial, fields, cholesky)
    return advanced, log_importance


def solution(mesh):
    in_specs = (
        P(("walk", "pair"), None, None),
        P(("walk", "pair"), None, None),
        P(None, "walk"),
        P(("walk", "pair"), None),
        P("pair", "walk", None),
    )
    out_specs = (P(("walk", "pair"), None, None), P(("walk", "pair")))
    return jax.shard_map(
        per_device, mesh=mesh, in_specs=in_specs, out_specs=out_specs, check_vma=False
    )
```

time: 484 us -> 118 us (0.24)
  waiting for transfers between devices: 401 us -> 0 us
  Pallas kernels: 0 us -> 115 us
  matrix products: 24.5 us -> 0 us
  blocking collectives: 16.8 us -> 0 us
  local copies, waits for them, and re-layouts: 17.4 us -> 2.8 us
  between operations: 13.9 us -> 0.64 us
  starting transfers between devices: 7.66 us -> 0 us
    all_gather x2 -> x0, waiting for transfers between devices: 224 us -> none  [the longest x1 192 us: per_device(): shifted = lax.all_gather(own_shifted, ('walk', 'pair'), axis=0, tiled=True)]
    unnamed x4 -> x0, waiting for transfers between devices: 159 us -> none
    pallas_call x0 -> x1, Pallas kernels: none -> 115 us  [per_device(): pl.pallas_call(kernel, out_shape=(jax.ShapeDtypeStruct(walkers.shape, F32...]
    dot_general x9 -> x0, matrix products: 24.5 us -> none  [the longest x1 11 us: per_device(): jnp.dot(greens, flat_slab, preferred_element_type=jnp.float32)]
    all_to_all x1 -> x0, waiting for transfers between devices: 18.3 us -> none  [per_device(): lax.all_to_all(blocks, ('walk', 'pair'), split_axis=0, concat_axis=0, til...]
    all_to_all x1 -> x0, blocking collectives: 16.8 us -> none  [per_device(): lax.all_to_all(rotated, 'pair', split_axis=1, concat_axis=0, tiled=True)]
    unnamed x13 -> x2, local copies, waits for them, and re-layouts: 10.9 us -> 2.8 us
    all_to_all x1 -> x0, starting transfers between devices: 7.53 us -> none  [per_device(): lax.all_to_all(blocks, ('walk', 'pair'), split_axis=0, concat_axis=0, til...]
  transfers between devices with their start and end apart: 4 -> 0, of which waited for: 4 -> 0; matrix products, arithmetic and copies ran while one was open for 0% -> 0% of each run, Pallas kernels for 0% -> 0%
where the time goes in v1:
time: 118 us
  Pallas kernels  115 us (97%)
  local copies, waits for them, and re-layouts  2.8 us (2%)
    pallas_call x1, Pallas kernels, per_device(): pl.pallas_call(kernel, out_shape=(jax.ShapeDtypeStruct(walkers.shape, F32...  115 us
    unnamed x2, local copies, waits for them, and re-layouts  2.8 us

profile of v1, /device:TPU:1, one launch (start us, length us, event | category | flops | bytes accessed | tf_op | source)
XLA Modules:
  0.0 118.1 jit_solution(16882353773269758836)
XLA Ops:
  0.6 114.7 %shard_map.68 = (f32[2,64,512]{2,1,0:T(8,128)}, f32[2]{0:T(128)}) custom-call(f32[2,64,512]{2,1,0:T(8,128)} %walkers.1, f32[2,64,64]{2,1,0:T(8,128)} %inverse.1, bf16[64,64]{1,0:T(8,128)(2,1)} %trial.1, f32[2,4096]{1,0:T(2,128)} %fields.1, bf16[32,64,4096]{2,1,0:T(8,128)(2,1)} %cholesky.1), custom_call_target="tpu_custom_call" | custom-call | tf_op jit(solution)/shard_map/pallas_call | solution.py:383
  115.3 1.7 %copy.9 = f32[2,64,512]{2,1,0:T(8,128)} copy(f32[2,64,512]{2,1,0:T(8,128)} %get-tuple-element.4) | data formatting | bytes 524288
  117.0 1.1 copy.10

commit v2 on v1

--- a/solution.py
+++ b/solution.py
@@ -98,6 +98,21 @@
                 row = fields[pl.ds(k, 1), pl.ds((n * 8 + to) * 128, 128)]
                 fields_out[to, pl.ds(k * 4 + n, 1), :] = row
 
+    square = jnp.concatenate([trial[...].astype(F32)] * 4, axis=0)
+    square = jnp.concatenate([square] * 4, axis=1)
+    rows = lax.broadcasted_iota(jnp.int32, (256, 256), 0) // 64
+    cols = lax.broadcasted_iota(jnp.int32, (256, 256), 1) // 64
+    diag[...] = jnp.where(rows == cols, square, 0.0).astype(BF16)
+
+    def rotate_group(g, carry):
+        block = pl.ds(pl.multiple_of(g * 256, 256), 256)
+        wait(slab.at[block], slab_sem.at[g])
+
+        half[block] = jnp.dot(diag[...], slab[block], preferred_element_type=F32).astype(BF16)
+        return carry
+
+    lax.fori_loop(0, 8, rotate_group, 0)
+
     pl.semaphore_wait(barrier, 127)
 
     def send_rotated(i, carry):
@@ -124,27 +139,6 @@
     lax.fori_loop(1, 8, send_fields, 0)
     fields_in[pl.ds(pl.multiple_of(a * 8, 8), 8)] = fields_out[a]
 
-    square = jnp.concatenate([trial[...].astype(F32)] * 4, axis=0)
-    square = jnp.concatenate([square] * 4, axis=1)
-    rows = lax.broadcasted_iota(jnp.int32, (256, 256), 0) // 64
-    cols = lax.broadcasted_iota(jnp.int32, (256, 256), 1) // 64
-    diag[...] = jnp.where(rows == cols, square, 0.0).astype(BF16)
-
-    def rotate_group(g, carry):
-        block = pl.ds(pl.multiple_of(g * 256, 256), 256)
-        wait(slab.at[block], slab_sem.at[g])
-
-        def columns(t, carry):
-            lanes = pl.ds(pl.multiple_of(t * 256, 256), 256)
-            half[block, lanes] = jnp.dot(
-                diag[...], slab[block, lanes], preferred_element_type=F32
-            ).astype(BF16)
-            return carry
-
-        return lax.fori_loop(0, 16, columns, carry)
-
-    lax.fori_loop(0, 8, rotate_group, 0)
-
     wait(recv_a.at[pl.ds(0, 127)], recv_sem.at[0])
 
     def regroup(g, carry):
@@ -162,17 +156,14 @@
         return hop_send.at[n * 6 + stage], hop_recv.at[n * 6 + stage]
 
     def bias_chunk(n):
-        def columns(t, carry):
-            lanes = pl.ds(pl.multiple_of(n * 1024 + t * 256, 256), 256)
-            got = jnp.dot(left[...], half[:, lanes], preferred_element_type=F32).astype(BF16)
-            for group in range(16):
-                for lane in range(2):
-                    parts[n, group // 8, (group // 2) % 4, group % 2, t, lane] = got[
-                        group * 16 : group * 16 + 16, lane * 128 : lane * 128 + 128
-                    ]
-            return carry
-
-        lax.fori_loop(0, 4, columns, 0)
+        got = jnp.dot(
+            left[...], half[:, pl.ds(n * 1024, 1024)], preferred_element_type=F32
+        ).astype(BF16)
+        for group in range(16):
+            for lane in range(8):
+                parts[n, group // 8, (group // 2) % 4, group % 2, lane // 2, lane % 2] = got[
+                    group * 16 : group * 16 + 16, lane * 128 : lane * 128 + 128
+                ]
         send(parts.at[n, 1 - c], from_core.at[n], hop(n, 0), (x, y, zh, zl, 1 - c))
 
     def add_core(n):
@@ -255,25 +246,24 @@
         wait(shifted.at[n, 1 - c], hop_recv.at[n * 6 + 5])
 
         def columns(t, carry):
-            block = pl.ds(pl.multiple_of(t * 256, 256), 256)
-            got = jnp.zeros((256, 256), F32) if n == 0 else total[t]
-            for i in range(4):
-                both = [shifted[n, :, :, :, i, lane].reshape(256, 128) for lane in range(2)]
-                got = got + lax.dot_general(
-                    jnp.concatenate(both, axis=1),
-                    slab[block, pl.ds(n * 1024 + i * 256, 256)],
-                    (((1,), (1,)), ((), ())), preferred_element_type=F32,
-                )
+            block = pl.ds(pl.multiple_of(t * 1024, 1024), 1024)
+            lanes = [shifted[n, :, :, :, i // 2, i % 2].reshape(256, 128) for i in range(8)]
+            got = lax.dot_general(
+                jnp.concatenate(lanes, axis=1), slab[block, pl.ds(n * 1024, 1024)],
+                (((1,), (1,)), ((), ())), preferred_element_type=F32,
+            )
+            if n > 0:
+                got = got + total[t]
             if n < CHUNKS - 1:
                 total[t] = got
             else:
-                for lane in range(2):
-                    wide[pl.ds(t * 2 + lane, 256, stride=16), :] = got[
+                for lane in range(8):
+                    wide[pl.ds(t * 8 + lane, 256, stride=16), :] = got[
                         :, lane * 128 : lane * 128 + 128
                     ]
             return carry
 
-        lax.fori_loop(0, 8, columns, 0)
+        lax.fori_loop(0, 2, columns, 0)
 
     steps = (bias_chunk, add_core, add_first, shift, spread_plane, spread_core, potential_chunk)
     for time in range(len(steps) + CHUNKS - 1):
@@ -366,7 +356,7 @@
         pltpu.VMEM((CHUNKS,) + chunk, BF16),
         pltpu.VMEM((CHUNKS, 15) + tile, BF16),
         pltpu.VMEM((CHUNKS, 2) + chunk, BF16),
-        pltpu.VMEM((8, 256, 256), F32),
+        pltpu.VMEM((2, 256, 1024), F32),
         pltpu.VMEM((128, 2) + tile, BF16),
         pltpu.VMEM((16, 8, 2) + tile, BF16),
         pltpu.VMEM((2, 512, 512), BF16),

time: 118 us -> 109 us (0.924)
  Pallas kernels: 115 us -> 105 us
    pallas_call x1, Pallas kernels: 115 us -> 105 us  [per_device(): pl.pallas_call(kernel, out_shape=(jax.ShapeDtypeStruct(walkers.shape, F32...]
where the time goes in v2:
time: 109 us; the launch traced here: 108 us
  Pallas kernels  105 us (96%)
  local copies, waits for them, and re-layouts  2.8 us (3%)
    pallas_call x1, Pallas kernels, per_device(): pl.pallas_call(kernel, out_shape=(jax.ShapeDtypeStruct(walkers.shape, F32...  105 us
    unnamed x2, local copies, waits for them, and re-layouts  2.8 us

profile of v2, /device:TPU:1, one launch (start us, length us, event | category | flops | bytes accessed | tf_op | source)
XLA Modules:
  0.0 108.4 jit_solution(8168933546039172885)
XLA Ops:
  0.6 105.0 %shard_map.68 = (f32[2,64,512]{2,1,0:T(8,128)}, f32[2]{0:T(128)}) custom-call(f32[2,64,512]{2,1,0:T(8,128)} %walkers.1, f32[2,64,64]{2,1,0:T(8,128)} %inverse.1, bf16[64,64]{1,0:T(8,128)(2,1)} %trial.1, f32[2,4096]{1,0:T(2,128)} %fields.1, bf16[32,64,4096]{2,1,0:T(8,128)(2,1)} %cholesky.1), custom_call_target="tpu_custom_call" | custom-call | tf_op jit(solution)/shard_map/pallas_call | solution.py:373
  105.6 1.7 %copy.9 = f32[2,64,512]{2,1,0:T(8,128)} copy(f32[2,64,512]{2,1,0:T(8,128)} %get-tuple-element.4) | data formatting | bytes 524288
  107.3 1.1 %copy.10 = f32[2]{0:T(128)} copy(f32[2]{0:T(128)} %get-tuple-element.5) | data formatting | bytes 16

commit v3 on v2

v3 whole, which is shorter than its diff:
```python
import functools

import jax
import jax.numpy as jnp
from jax import lax
from jax.experimental import pallas as pl
from jax.experimental.pallas import tpu as pltpu
from jax.sharding import PartitionSpec as P

MESH = pl.DeviceIdType.MESH
F32 = jnp.float32
BF16 = jnp.bfloat16
time_root = 0.1
CHUNKS = 4
STAGES = 3
FIRST_AXIS = ("x", "y", "z", "x")
REST = {"x": (4, 2, 2), "y": (2, 4, 2), "z": (4, 4)}


def device_of(pos):
    x, y, zh, zl, c = pos
    return (x * 2 + zl, (y * 2 + zh) * 2 + c)


def moved(pos, axis, d):
    x, y, zh, zl, c = pos
    if axis == "x":
        return (lax.rem(x + d, 4), y, zh, zl, c)
    if axis == "y":
        return (x, lax.rem(y + d, 4), zh, zl, c)
    z = lax.rem(zh * 2 + zl + d, 4)
    return (x, y, z // 2, lax.rem(z, 2), c)


def slab_index(axis, pos):
    x, y, zh, zl, _ = pos
    every = slice(None)
    return {"x": (every, every, x), "y": (y,), "z": (every, zh, every, zl)}[axis]


def tile_index(axis, pos):
    x, y, zh, zl, _ = pos
    return {"x": (y, zh, zl), "y": (zh, x, zl), "z": (y, x)}[axis]


def kernel(
    walkers, inverse, trial, fields, cholesky, out, log_out,
    stage, half, turned, diag, send_a, recv_a, pass_a, wide, left, fields_out, fields_in,
    parts, from_core, sums, shifted, moved_fields, total, send_d, recv_d, pass_d, potential,
    logs, logs_in, *rest,
):
    first_in = rest[:CHUNKS]
    first_sum = rest[CHUNKS : 2 * CHUNKS]
    slab_sem, send_sem, recv_sem, hop_send, hop_recv = rest[2 * CHUNKS :]
    a, b = lax.axis_index("walk"), lax.axis_index("pair")
    x, zl = a // 2, lax.rem(a, 2)
    c = lax.rem(b, 2)
    y, zh = b // 4, lax.rem(b // 2, 2)
    here = (x, y, zh, zl, c)
    sibling = (x, y, zh, zl, 1 - c)

    def chip_of(pos):
        return (pos[1] * 2 + pos[2]) * 8 + pos[0] * 2 + pos[3]

    chip = chip_of(here)

    def other(i):
        i = lax.rem(i * 37, 64)
        pos = moved(here, "x", lax.rem(i, 4))
        return moved(moved(pos, "y", lax.rem(i // 4, 4)), "z", i // 16)

    def walk_peer(i):
        return (lax.rem(x + i // 2, 4), y, zh, lax.rem(zl + i, 2), c)

    def plane_peer(axis, i):
        one, two = {"x": ("y", "z"), "y": ("z", "x"), "z": ("x", "y")}[axis]
        return moved(moved(here, one, i // 4), two, lax.rem(i, 4))

    def send(src, dst, sems, pos):
        pltpu.make_async_remote_copy(
            src_ref=src, dst_ref=dst, send_sem=sems[0], recv_sem=sems[1],
            device_id=device_of(pos), device_id_type=MESH,
        ).start()

    def wait(ref, sem):
        pltpu.make_async_copy(ref, ref, sem).wait()

    def pair_sems(i):
        return send_sem.at[i], recv_sem.at[i]

    def hop(n, step):
        return hop_send.at[n * 6 + step], hop_recv.at[n * 6 + step]

    def load(g):
        for q in range(4):
            pltpu.make_async_copy(
                cholesky.at[(q % 2) * 16 + g * 2 + q // 2],
                stage.at[lax.rem(g, STAGES), pl.ds(q * 64, 64)],
                slab_sem.at[g],
            ).start()

    barrier = pltpu.get_barrier_semaphore()

    def greet(i, carry):
        pl.semaphore_signal(barrier, inc=1, device_id=device_of(other(i)), device_id_type=MESH)
        return carry

    pl.semaphore_signal(barrier, inc=1, device_id=device_of(sibling), device_id_type=MESH)
    lax.fori_loop(1, 64, greet, 0)

    for g in range(STAGES):
        load(jnp.int32(g))

    for k in range(2):
        flipped = jnp.transpose(walkers[k])
        rotated = jnp.dot(
            flipped, inverse[k], precision=lax.Precision.HIGHEST, preferred_element_type=F32
        )
        rotated = rotated.reshape(16, 2, 16, 64)
        rotated = jnp.concatenate([rotated[:, 0], rotated[:, 1]], axis=-1).astype(BF16)
        send_a[k] = rotated.reshape(8, 2, 16, 128)

    pl.semaphore_wait(barrier, 64)

    for k in range(2):

        def send_rotated(i, carry, k=k):
            pos = other(i)
            src = send_a.at[k, pos[1] * 2 + pos[2]]
            send(src, recv_a.at[k, :, chip], pair_sems(k), pos)
            return carry

        lax.fori_loop(1, 64, send_rotated, 0)
        recv_a[k, :, chip] = send_a[k, y * 2 + zh]

    for k in range(2):
        for to in range(8):
            for lane in range(4):
                at = (lane // 2) * 2048 + to * 256 + (lane % 2) * 128
                fields_out[to, pl.ds(k * 4 + lane, 1), :] = fields[pl.ds(k, 1), pl.ds(at, 128)]
    mine = pl.ds(pl.multiple_of(a * 8, 8), 8)

    def send_fields(i, carry):
        pos = walk_peer(i)
        send(fields_out.at[device_of(pos)[0]], fields_in.at[mine], pair_sems(2), pos)
        return carry

    lax.fori_loop(1, 8, send_fields, 0)
    fields_in[mine] = fields_out[a]

    square = jnp.concatenate([trial[...].astype(F32)] * 4, axis=0)
    square = jnp.concatenate([square] * 4, axis=1)
    rows = lax.broadcasted_iota(jnp.int32, (256, 256), 0) // 64
    cols = lax.broadcasted_iota(jnp.int32, (256, 256), 1) // 64
    diag[...] = jnp.where(rows == cols, square, 0.0).astype(BF16)

    for g in range(8):
        block = pl.ds(g * 256, 256)
        wait(stage.at[g % STAGES], slab_sem.at[g])
        half[block] = jnp.dot(
            diag[...], stage[g % STAGES], preferred_element_type=F32
        ).astype(BF16)
        turned[:, block] = jnp.transpose(stage[g % STAGES])
        if g + STAGES < 8:
            load(jnp.int32(g + STAGES))

    def regroup(k, side, source):
        def some(g, carry):
            base = pl.multiple_of(side * 1024 + g * 256, 256)
            wide[pl.ds(base, 256), :] = source[pl.ds(g * 16, 16)].astype(F32).reshape(256, 128)
            for j in range(16):
                left[
                    k, pl.ds(pl.multiple_of(side * 64 + g * 16, 16), 16), pl.ds(j * 128, 128)
                ] = wide[pl.ds(base + j, 16, stride=16), :].astype(BF16)
            return carry

        lax.fori_loop(0, 4, some, 0)

    def receive(k):
        wait(recv_a.at[k, :, pl.ds(0, 63)], recv_sem.at[k])
        send(recv_a.at[k, 1 - c], pass_a.at[k], pair_sems(3 + k), sibling)
        regroup(k, 0, recv_a.at[k, c])
        wait(pass_a.at[k], recv_sem.at[3 + k])
        regroup(k, 1, pass_a.at[k])

    def bias_chunk(n):
        got = jnp.dot(
            left[n // 2], half[:, pl.ds((n % 2) * 2048, 2048)], preferred_element_type=F32
        )
        for group in range(16):
            for to in range(8):
                tile = [
                    got[group * 8 : group * 8 + 8, at * 128 : at * 128 + 128]
                    for at in (to * 2, to * 2 + 1)
                ]
                parts[n, group // 8, (group // 2) % 4, group % 2, to // 2, to % 2] = (
                    jnp.concatenate(tile, axis=0).astype(BF16)
                )
        send(parts.at[n, 1], from_core.at[n], hop(n, 0), sibling)

    def add_core(n):
        wait(from_core.at[n], hop_recv.at[n * 6])

        def add(i, carry):
            both = parts[n, 0, i].astype(F32) + from_core[n, i].astype(F32)
            parts[n, 0, i] = both.astype(BF16)
            return carry

        lax.fori_loop(0, 4, add, 0)
        axis = FIRST_AXIS[n]
        for d in (2, 1, 3):
            pos = moved(here, axis, d)
            src = parts.at[(n, 0) + slab_index(axis, pos)]
            send(src, first_in[n].at[d - 1], hop(n, 1), pos)

    def add_first(n):
        axis = FIRST_AXIS[n]
        wait(first_in[n], hop_recv.at[n * 6 + 1])
        got = parts[(n, 0) + slab_index(axis, here)].astype(F32)
        for d in range(3):
            got = got + first_in[n][d].astype(F32)
        first_sum[n][...] = got.astype(BF16)

        def give(i, carry):
            pos = plane_peer(axis, i)
            send(first_sum[n].at[tile_index(axis, pos)], sums.at[n, i - 1], hop(n, 2), pos)
            return carry

        lax.fori_loop(1, 16, give, 0)

    def shift(n):
        axis = FIRST_AXIS[n]
        if n == 0:
            wait(fields_in.at[pl.ds(0, 56)], recv_sem.at[2])
        wait(sums.at[n], hop_recv.at[n * 6 + 2])
        bias = first_sum[n][tile_index(axis, here)].astype(F32)
        for i in range(15):
            bias = bias + sums[n, i].astype(F32)
        bias_shift = -time_root * bias
        field = jnp.concatenate(
            [fields_in[pl.ds(n * 2 + lane, 8, stride=8), :] for lane in range(2)], axis=0
        )
        place = (n, 0, y, zh, x, zl)
        shifted[place] = (field - bias_shift).astype(BF16)

        def give(i, carry):
            send(shifted.at[place], shifted.at[place], hop(n, 3), plane_peer(axis, i))
            return carry

        lax.fori_loop(1, 16, give, 0)
        term = field * bias_shift - 0.5 * bias_shift * bias_shift
        term = term[:8] + term[8:]
        rows = pl.ds((n // 2) * 8, 8)
        logs[rows] = term if n % 2 == 0 else logs[rows] + term
        if n == CHUNKS - 1:
            logs_in[a] = logs[...]

            def give_logs(i, carry):
                send(logs, logs_in.at[a], pair_sems(5), walk_peer(i))
                return carry

            lax.fori_loop(1, 8, give_logs, 0)

    def spread_plane(n):
        axis = FIRST_AXIS[n]
        wait(sums.at[n], hop_recv.at[n * 6 + 3])
        part = shifted.at[(n, 0) + slab_index(axis, here)]
        for d in (2, 1, 3):
            send(part, part, hop(n, 4), moved(here, axis, d))

    def spread_core(n):
        wait(first_in[n], hop_recv.at[n * 6 + 4])
        send(shifted.at[n, 0], shifted.at[n, 1], hop(n, 5), sibling)

    def potential_chunk(n):
        wait(shifted.at[n, 1], hop_recv.at[n * 6 + 5])
        for at in range(8):
            tiles = shifted[n, :, :, :, at // 2, at % 2].astype(F32).reshape(16, 16, 128)
            for lane in range(2):
                moved_fields[:, pl.ds((at * 2 + lane) * 128, 128)] = (
                    tiles[:, lane * 8 : lane * 8 + 8].reshape(128, 128).astype(BF16)
                )
        got = jnp.dot(
            moved_fields[...], turned[pl.ds((n % 2) * 2048, 2048)], preferred_element_type=F32
        )
        if n % 2 == 0:
            total[...] = got
        else:
            got = got + total[...]
            for j in range(16):
                wide[pl.ds(j, 128, stride=16), :] = got[:, j * 128 : j * 128 + 128]

    def give_potential(k):
        for side in range(2):

            def narrow(g, carry, side=side):
                block = wide[pl.ds(pl.multiple_of(side * 1024 + g * 256, 256), 256), :]
                send_d[k, pl.ds(g * 16, 16), side] = block.astype(BF16).reshape(16, 16, 128)
                return carry

            lax.fori_loop(0, 4, narrow, 0)

        def give(i, carry):
            pos = other(i)
            send(send_d.at[k, chip_of(pos)], recv_d.at[k, :, chip], pair_sems(6 + k), pos)
            return carry

        lax.fori_loop(1, 64, give, 0)
        recv_d[k, :, chip] = send_d[k, chip]

    def pass_potential(k):
        wait(recv_d.at[k, :, pl.ds(0, 63)], recv_sem.at[6 + k])
        send(recv_d.at[k, 1], pass_d.at[k], pair_sems(8 + k), sibling)

    def assemble(k, core, source):
        def some(i, carry):
            for h in range(2):
                row = pl.multiple_of((i * 2 + core) * 32 + h * 16, 16)
                for pair in range(4):
                    both = [
                        source[i * 8 + pair * 2 + e].astype(F32)[:, h * 64 : h * 64 + 64]
                        for e in range(2)
                    ]
                    potential[k, pl.ds(row, 16), pl.ds(pair * 128, 128)] = jnp.concatenate(
                        both, axis=1
                    ).astype(BF16)
            return carry

        lax.fori_loop(0, 8, some, 0)

    def propagate(k):
        assemble(k, c, recv_d.at[k, 0])
        wait(pass_d.at[k], recv_sem.at[8 + k])
        assemble(k, 1 - c, pass_d.at[k])
        series_term = walkers[k]
        summed = series_term
        for degree in range(1, 7):
            product = lax.dot_general(
                series_term.astype(BF16), potential[k], (((1,), (1,)), ((), ())),
                preferred_element_type=F32,
            )
            series_term = product * (-time_root / degree)
            summed = summed + series_term
        out[k] = summed

    receive(0)
    bias_chunk(0)
    bias_chunk(1)
    add_core(0)
    add_core(1)
    receive(1)
    bias_chunk(2)
    bias_chunk(3)
    add_first(0)
    add_first(1)
    add_core(2)
    add_core(3)
    shift(0)
    shift(1)
    add_first(2)
    add_first(3)
    spread_plane(0)
    spread_plane(1)
    shift(2)
    shift(3)
    spread_core(0)
    spread_core(1)
    spread_plane(2)
    spread_plane(3)
    potential_chunk(0)
    potential_chunk(1)
    give_potential(0)
    spread_core(2)
    spread_core(3)
    potential_chunk(2)
    potential_chunk(3)
    give_potential(1)
    pass_potential(0)
    propagate(0)

    wait(logs_in.at[pl.ds(0, 7)], recv_sem.at[5])
    all_logs = logs_in[0]
    for i in range(1, 8):
        all_logs = all_logs + logs_in[i]
    log_rows = lax.broadcasted_iota(jnp.int32, (16, 128), 0)
    for k in range(2):
        log_out[k] = jnp.sum(jnp.where(log_rows == k * 8 + a, all_logs, 0.0))

    pass_potential(1)
    propagate(1)

    for k in range(2):
        wait(recv_a.at[k, :, pl.ds(0, 63)], send_sem.at[k])
        wait(recv_d.at[k, :, pl.ds(0, 63)], send_sem.at[6 + k])
        wait(pass_a.at[k], send_sem.at[3 + k])
        wait(pass_d.at[k], send_sem.at[8 + k])
    wait(fields_in.at[pl.ds(0, 56)], send_sem.at[2])
    wait(logs_in.at[pl.ds(0, 7)], send_sem.at[5])
    for n in range(CHUNKS):
        for step, size in enumerate(
            (from_core.at[n], first_in[n], sums.at[n], sums.at[n], first_in[n], from_core.at[n])
        ):
            wait(size, hop_send.at[n * 6 + step])


def per_device(walkers, inverse_intersection, trial, fields, cholesky):
    vmem = pl.BlockSpec(memory_space=pltpu.VMEM)
    tile = (16, 128)
    chunk = (4, 2, 4, 2) + tile
    scratch = [
        pltpu.VMEM((STAGES, 256, 4096), BF16),
        pltpu.VMEM((2048, 4096), BF16),
        pltpu.VMEM((4096, 2048), BF16),
        pltpu.VMEM((256, 256), BF16),
        pltpu.VMEM((2, 8, 2) + tile, BF16),
        pltpu.VMEM((2, 2, 64) + tile, BF16),
        pltpu.VMEM((2, 64) + tile, BF16),
        pltpu.VMEM((2048, 128), F32),
        pltpu.VMEM((2, 128, 2048), BF16),
        pltpu.VMEM((8, 8, 128), F32),
        pltpu.VMEM((64, 128), F32),
        pltpu.VMEM((CHUNKS, 2) + chunk, BF16),
        pltpu.VMEM((CHUNKS,) + chunk, BF16),
        pltpu.VMEM((CHUNKS, 15) + tile, BF16),
        pltpu.VMEM((CHUNKS, 2) + chunk, BF16),
        pltpu.VMEM((128, 2048), BF16),
        pltpu.VMEM((128, 2048), F32),
        pltpu.VMEM((2, 64, 2) + tile, BF16),
        pltpu.VMEM((2, 2, 64) + tile, BF16),
        pltpu.VMEM((2, 64) + tile, BF16),
        pltpu.VMEM((2, 512, 512), BF16),
        pltpu.VMEM(tile, F32),
        pltpu.VMEM((8,) + tile, F32),
        *[pltpu.VMEM((3,) + REST[axis] + tile, BF16) for axis in FIRST_AXIS],
        *[pltpu.VMEM(REST[axis] + tile, BF16) for axis in FIRST_AXIS],
        pltpu.SemaphoreType.DMA((8,)),
        pltpu.SemaphoreType.DMA((10,)),
        pltpu.SemaphoreType.DMA((10,)),
        pltpu.SemaphoreType.DMA((CHUNKS * 6,)),
        pltpu.SemaphoreType.DMA((CHUNKS * 6,)),
    ]
    advanced, log_importance = pl.pallas_call(
        kernel,
        out_shape=(
            jax.ShapeDtypeStruct(walkers.shape, F32),
            jax.ShapeDtypeStruct((2,), F32),
        ),
        in_specs=[vmem, vmem, vmem, vmem, pl.BlockSpec(memory_space=pl.ANY)],
        out_specs=(vmem, pl.BlockSpec(memory_space=pltpu.SMEM)),
        scratch_shapes=scratch,
        compiler_params=pltpu.CompilerParams(
            collective_id=0, has_side_effects=True, vmem_limit_bytes=62 * 1024 * 1024
        ),
    )(walkers, inverse_intersection, trial, fields, cholesky)
    return advanced, log_importance


def solution(mesh):
    in_specs = (
        P(("walk", "pair"), None, None),
        P(("walk", "pair"), None, None),
        P(None, "walk"),
        P(("walk", "pair"), None),
        P("pair", "walk", None),
    )
    out_specs = (P(("walk", "pair"), None, None), P(("walk", "pair")))
    return jax.shard_map(
        per_device, mesh=mesh, in_specs=in_specs, out_specs=out_specs, check_vma=False
    )
```

time: 109 us -> 77 us (0.71)
  Pallas kernels: 105 us -> 73.4 us
    pallas_call x1, Pallas kernels: 105 us -> 73.4 us  [per_device(): pl.pallas_call(kernel, out_shape=(jax.ShapeDtypeStruct(walkers.shape, F32...]
where the time goes in v3:
time: 77 us; the launch traced here: 76.9 us
  Pallas kernels  73.4 us (95%)
  local copies, waits for them, and re-layouts  2.8 us (4%)
    pallas_call x1, Pallas kernels, per_device(): pl.pallas_call(kernel, out_shape=(jax.ShapeDtypeStruct(walkers.shape, F32...  73.4 us
    unnamed x2, local copies, waits for them, and re-layouts  2.8 us

profile of v3, /device:TPU:1, one launch (start us, length us, event | category | flops | bytes accessed | tf_op | source)
XLA Modules:
  0.0 76.9 jit_solution(15132933373905840362)
XLA Ops:
  0.6 73.4 %shard_map.68 = (f32[2,64,512]{2,1,0:T(8,128)}, f32[2]{0:T(128)}) custom-call(f32[2,64,512]{2,1,0:T(8,128)} %walkers.1, f32[2,64,64]{2,1,0:T(8,128)} %inverse.1, bf16[64,64]{1,0:T(8,128)(2,1)} %trial.1, f32[2,4096]{1,0:T(2,128)} %fields.1, bf16[32,64,4096]{2,1,0:T(8,128)(2,1)} %cholesky.1), custom_call_target="tpu_custom_call" | custom-call | tf_op jit(solution)/shard_map/pallas_call | solution.py:442
  74.1 1.7 %copy.9 = f32[2,64,512]{2,1,0:T(8,128)} copy(f32[2,64,512]{2,1,0:T(8,128)} %get-tuple-element.4) | data formatting | bytes 524288
  75.7 1.1 %copy.10 = f32[2]{0:T(128)} copy(f32[2]{0:T(128)} %get-tuple-element.5) | data formatting | bytes 16

commit v4 on v3

--- a/solution.py
+++ b/solution.py
@@ -13,6 +13,7 @@
 time_root = 0.1
 CHUNKS = 4
 STAGES = 3
+FARTHEST = sorted(range(1, 16), key=lambda i: -min(i // 4, 4 - i // 4) - min(i % 4, 4 - i % 4))
 FIRST_AXIS = ("x", "y", "z", "x")
 REST = {"x": (4, 2, 2), "y": (2, 4, 2), "z": (4, 4)}
 
@@ -44,14 +45,14 @@
 
 
 def kernel(
-    walkers, inverse, trial, fields, cholesky, out, log_out,
-    stage, half, turned, diag, send_a, recv_a, pass_a, wide, left, fields_out, fields_in,
+    walkers_in, inverse_in, trial, fields, cholesky, out, log_out,
+    walkers, inverse, stage, half, turned, diag, send_a, recv_a, pass_a, wide, left, fields_out, fields_in,
     parts, from_core, sums, shifted, moved_fields, total, send_d, recv_d, pass_d, potential,
     logs, logs_in, *rest,
 ):
     first_in = rest[:CHUNKS]
     first_sum = rest[CHUNKS : 2 * CHUNKS]
-    slab_sem, send_sem, recv_sem, hop_send, hop_recv = rest[2 * CHUNKS :]
+    in_sem, slab_sem, send_sem, recv_sem, hop_send, hop_recv = rest[2 * CHUNKS :]
     a, b = lax.axis_index("walk"), lax.axis_index("pair")
     x, zl = a // 2, lax.rem(a, 2)
     c = lax.rem(b, 2)
@@ -69,12 +70,21 @@
         pos = moved(here, "x", lax.rem(i, 4))
         return moved(moved(pos, "y", lax.rem(i // 4, 4)), "z", i // 16)
 
+    xs = [lax.rem(x + d, 4) for d in range(4)]
+    ys = [lax.rem(y + d, 4) for d in range(4)]
+    zs = [lax.rem(zh * 2 + zl + d, 4) for d in range(4)]
+    far = [
+        (xs[i % 4], ys[i // 4 % 4], zs[i // 16] // 2, lax.rem(zs[i // 16], 2), c)
+        for i in range(64)
+    ]
+
     def walk_peer(i):
         return (lax.rem(x + i // 2, 4), y, zh, lax.rem(zl + i, 2), c)
 
     def plane_peer(axis, i):
-        one, two = {"x": ("y", "z"), "y": ("z", "x"), "z": ("x", "y")}[axis]
-        return moved(moved(here, one, i // 4), two, lax.rem(i, 4))
+        one, two = i // 4, i % 4
+        dx, dy, dz = {"x": (0, one, two), "y": (two, 0, one), "z": (one, two, 0)}[axis]
+        return far[dx + dy * 4 + dz * 16]
 
     def send(src, dst, sems, pos):
         pltpu.make_async_remote_copy(
@@ -100,18 +110,15 @@
             ).start()
 
     barrier = pltpu.get_barrier_semaphore()
-
-    def greet(i, carry):
-        pl.semaphore_signal(barrier, inc=1, device_id=device_of(other(i)), device_id_type=MESH)
-        return carry
-
     pl.semaphore_signal(barrier, inc=1, device_id=device_of(sibling), device_id_type=MESH)
-    lax.fori_loop(1, 64, greet, 0)
-
-    for g in range(STAGES):
-        load(jnp.int32(g))
-
-    for k in range(2):
+    pltpu.make_async_copy(walkers_in, walkers, in_sem.at[0]).start()
+    pltpu.make_async_copy(inverse_in, inverse, in_sem.at[1]).start()
+    for i in range(1, 64):
+        pl.semaphore_signal(
+            barrier, inc=1, device_id=device_of(far[i * 37 % 64]), device_id_type=MESH
+        )
+
+    def rotate(k):
         flipped = jnp.transpose(walkers[k])
         rotated = jnp.dot(
             flipped, inverse[k], precision=lax.Precision.HIGHEST, preferred_element_type=F32
@@ -120,18 +127,25 @@
         rotated = jnp.concatenate([rotated[:, 0], rotated[:, 1]], axis=-1).astype(BF16)
         send_a[k] = rotated.reshape(8, 2, 16, 128)
 
-    pl.semaphore_wait(barrier, 64)
-
-    for k in range(2):
-
-        def send_rotated(i, carry, k=k):
+    def give_rotated(k):
+        def give(i, carry):
             pos = other(i)
             src = send_a.at[k, pos[1] * 2 + pos[2]]
             send(src, recv_a.at[k, :, chip], pair_sems(k), pos)
             return carry
 
-        lax.fori_loop(1, 64, send_rotated, 0)
+        lax.fori_loop(1, 64, give, 0)
         recv_a[k, :, chip] = send_a[k, y * 2 + zh]
+
+    for g in range(STAGES):
+        load(jnp.int32(g))
+    wait(walkers, in_sem.at[0])
+    wait(inverse, in_sem.at[1])
+    rotate(0)
+    pl.semaphore_wait(barrier, 64)
+    give_rotated(0)
+    rotate(1)
+    give_rotated(1)
 
     for k in range(2):
         for to in range(8):
@@ -154,15 +168,20 @@
     cols = lax.broadcasted_iota(jnp.int32, (256, 256), 1) // 64
     diag[...] = jnp.where(rows == cols, square, 0.0).astype(BF16)
 
-    for g in range(8):
-        block = pl.ds(g * 256, 256)
-        wait(stage.at[g % STAGES], slab_sem.at[g])
-        half[block] = jnp.dot(
-            diag[...], stage[g % STAGES], preferred_element_type=F32
-        ).astype(BF16)
-        turned[:, block] = jnp.transpose(stage[g % STAGES])
-        if g + STAGES < 8:
-            load(jnp.int32(g + STAGES))
+    def turn(g, carry):
+        block = pl.ds(pl.multiple_of(g * 256, 256), 256)
+        now = lax.rem(g, STAGES)
+        wait(stage.at[now], slab_sem.at[g])
+        half[block] = jnp.dot(diag[...], stage[now], preferred_element_type=F32).astype(BF16)
+        turned[:, block] = jnp.transpose(stage[now])
+
+        @pl.when(g + STAGES < 8)
+        def _():
+            load(g + STAGES)
+
+        return carry
+
+    lax.fori_loop(0, 8, turn, 0)
 
     def regroup(k, side, source):
         def some(g, carry):
@@ -221,12 +240,9 @@
             got = got + first_in[n][d].astype(F32)
         first_sum[n][...] = got.astype(BF16)
 
-        def give(i, carry):
+        for i in FARTHEST:
             pos = plane_peer(axis, i)
             send(first_sum[n].at[tile_index(axis, pos)], sums.at[n, i - 1], hop(n, 2), pos)
-            return carry
-
-        lax.fori_loop(1, 16, give, 0)
 
     def shift(n):
         axis = FIRST_AXIS[n]
@@ -243,11 +259,8 @@
         place = (n, 0, y, zh, x, zl)
         shifted[place] = (field - bias_shift).astype(BF16)
 
-        def give(i, carry):
+        for i in FARTHEST:
             send(shifted.at[place], shifted.at[place], hop(n, 3), plane_peer(axis, i))
-            return carry
-
-        lax.fori_loop(1, 16, give, 0)
         term = field * bias_shift - 0.5 * bias_shift * bias_shift
         term = term[:8] + term[8:]
         rows = pl.ds((n // 2) * 8, 8)
@@ -403,11 +416,20 @@
             wait(size, hop_send.at[n * 6 + step])
 
 
+def settle(result, log, out, log_out):
+    out[...] = result[...]
+    for k in range(2):
+        log_out[k] = log[k]
+
+
 def per_device(walkers, inverse_intersection, trial, fields, cholesky):
     vmem = pl.BlockSpec(memory_space=pltpu.VMEM)
+    whole = pl.BlockSpec(memory_space=pl.ANY)
     tile = (16, 128)
     chunk = (4, 2, 4, 2) + tile
     scratch = [
+        pltpu.VMEM(walkers.shape, F32),
+        pltpu.VMEM(inverse_intersection.shape, F32),
         pltpu.VMEM((STAGES, 256, 4096), BF16),
         pltpu.VMEM((2048, 4096), BF16),
         pltpu.VMEM((4096, 2048), BF16),
@@ -433,6 +455,7 @@
         pltpu.VMEM((8,) + tile, F32),
         *[pltpu.VMEM((3,) + REST[axis] + tile, BF16) for axis in FIRST_AXIS],
         *[pltpu.VMEM(REST[axis] + tile, BF16) for axis in FIRST_AXIS],
+        pltpu.SemaphoreType.DMA((2,)),
         pltpu.SemaphoreType.DMA((8,)),
         pltpu.SemaphoreType.DMA((10,)),
         pltpu.SemaphoreType.DMA((10,)),
@@ -445,14 +468,23 @@
             jax.ShapeDtypeStruct(walkers.shape, F32),
             jax.ShapeDtypeStruct((2,), F32),
         ),
-        in_specs=[vmem, vmem, vmem, vmem, pl.BlockSpec(memory_space=pl.ANY)],
+        in_specs=[whole, whole, vmem, vmem, whole],
         out_specs=(vmem, pl.BlockSpec(memory_space=pltpu.SMEM)),
         scratch_shapes=scratch,
         compiler_params=pltpu.CompilerParams(
             collective_id=0, has_side_effects=True, vmem_limit_bytes=62 * 1024 * 1024
         ),
     )(walkers, inverse_intersection, trial, fields, cholesky)
-    return advanced, log_importance
+    smem = pl.BlockSpec(memory_space=pltpu.SMEM)
+    return pl.pallas_call(
+        settle,
+        out_shape=(
+            jax.ShapeDtypeStruct(walkers.shape, F32),
+            jax.ShapeDtypeStruct((2,), F32),
+        ),
+        in_specs=[vmem, smem],
+        out_specs=(vmem, smem),
+    )(advanced, log_importance)
 
 
 def solution(mesh):

time: 77 us -> 75.6 us (0.982)
  local copies, waits for them, and re-layouts: 2.8 us -> 0 us
  Pallas kernels: 73.4 us -> 74.6 us
    unnamed x2 -> x0, local copies, waits for them, and re-layouts: 2.8 us -> none
    pallas_call x0 -> x1, Pallas kernels: none -> 1.69 us  [per_device(): pl.pallas_call(settle, out_shape=(jax.ShapeDtypeStruct(walkers.shape, F32...]
where the time goes in v4:
time: 75.6 us; the launch traced here: 75.4 us
  Pallas kernels  74.6 us (99%)
  between operations  0.8 us (1%)
    pallas_call x1, Pallas kernels, per_device(): pl.pallas_call(kernel, out_shape=(jax.ShapeDtypeStruct(walkers.shape, F32...  72.9 us
    pallas_call x1, Pallas kernels, per_device(): pl.pallas_call(settle, out_shape=(jax.ShapeDtypeStruct(walkers.shape, F32...  1.69 us

profile of v4, /device:TPU:1, one launch (start us, length us, event | category | flops | bytes accessed | tf_op | source)
XLA Modules:
  0.0 75.4 jit_solution(16448375205920823605)
XLA Ops:
  0.6 72.9 %shard_map.68 = (f32[2,64,512]{2,1,0:T(8,128)}, f32[2]{0:T(128)}) custom-call(f32[2,64,512]{2,1,0:T(8,128)} %walkers_in.1, f32[2,64,64]{2,1,0:T(8,128)} %inverse_in.1, bf16[64,64]{1,0:T(8,128)(2,1)} %trial.1, f32[2,4096]{1,0:T(2,128)} %fields.1, bf16[32,64,4096]{2,1,0:T(8,128)(2,1)} %cholesky.1), custom_call_target="tpu_custom_call" | custom-call | tf_op jit(solution)/shard_map/pallas_call | solution.py:465
  73.5 1.7 %shard_map.69 = (f32[2,64,512]{2,1,0:T(8,128)}, f32[2]{0:T(128)}) custom-call(f32[2,64,512]{2,1,0:T(8,128)} %get-tuple-element.4.result, f32[2]{0:T(128)} %get-tuple-element.5.log), custom_call_target="tpu_custom_call" | custom-call | tf_op jit(solution)/shard_map/pallas_call | solution.py:479

commit v5 on v4

--- a/solution.py
+++ b/solution.py
@@ -14,7 +14,7 @@
 CHUNKS = 4
 STAGES = 3
 FARTHEST = sorted(range(1, 16), key=lambda i: -min(i // 4, 4 - i // 4) - min(i % 4, 4 - i % 4))
-FIRST_AXIS = ("x", "y", "z", "x")
+FIRST_AXIS = ("x", "y", "x", "y")
 REST = {"x": (4, 2, 2), "y": (2, 4, 2), "z": (4, 4)}
 
 
@@ -65,11 +65,6 @@
 
     chip = chip_of(here)
 
-    def other(i):
-        i = lax.rem(i * 37, 64)
-        pos = moved(here, "x", lax.rem(i, 4))
-        return moved(moved(pos, "y", lax.rem(i // 4, 4)), "z", i // 16)
-
     xs = [lax.rem(x + d, 4) for d in range(4)]
     ys = [lax.rem(y + d, 4) for d in range(4)]
     zs = [lax.rem(zh * 2 + zl + d, 4) for d in range(4)]
@@ -128,13 +123,10 @@
         send_a[k] = rotated.reshape(8, 2, 16, 128)
 
     def give_rotated(k):
-        def give(i, carry):
-            pos = other(i)
+        for i in range(1, 64):
+            pos = far[i * 37 % 64]
             src = send_a.at[k, pos[1] * 2 + pos[2]]
             send(src, recv_a.at[k, :, chip], pair_sems(k), pos)
-            return carry
-
-        lax.fori_loop(1, 64, give, 0)
         recv_a[k, :, chip] = send_a[k, y * 2 + zh]
 
     for g in range(STAGES):
@@ -313,12 +305,9 @@
 
             lax.fori_loop(0, 4, narrow, 0)
 
-        def give(i, carry):
-            pos = other(i)
+        for i in range(1, 64):
+            pos = far[i * 37 % 64]
             send(send_d.at[k, chip_of(pos)], recv_d.at[k, :, chip], pair_sems(6 + k), pos)
-            return carry
-
-        lax.fori_loop(1, 64, give, 0)
         recv_d[k, :, chip] = send_d[k, chip]
 
     def pass_potential(k):

time: 75.6 us -> 72.6 us (0.960)
  Pallas kernels: 74.6 us -> 71.7 us
    pallas_call x1, Pallas kernels: 72.9 us -> 70 us  [per_device(): pl.pallas_call(kernel, out_shape=(jax.ShapeDtypeStruct(walkers.shape, F32...]
where the time goes in v5:
time: 72.6 us; the launch traced here: 72.4 us
  Pallas kernels  71.7 us (99%)
    pallas_call x1, Pallas kernels, per_device(): pl.pallas_call(kernel, out_shape=(jax.ShapeDtypeStruct(walkers.shape, F32...  70 us
    pallas_call x1, Pallas kernels, per_device(): pl.pallas_call(settle, out_shape=(jax.ShapeDtypeStruct(walkers.shape, F32...  1.69 us

profile of v5, /device:TPU:1, one launch (start us, length us, event | category | flops | bytes accessed | tf_op | source)
XLA Modules:
  0.0 72.4 jit_solution(3221366686790532090)
XLA Ops:
  0.6 70.0 %shard_map.68 = (f32[2,64,512]{2,1,0:T(8,128)}, f32[2]{0:T(128)}) custom-call(f32[2,64,512]{2,1,0:T(8,128)} %walkers_in.1, f32[2,64,64]{2,1,0:T(8,128)} %inverse_in.1, bf16[64,64]{1,0:T(8,128)(2,1)} %trial.1, f32[2,4096]{1,0:T(2,128)} %fields.1, bf16[32,64,4096]{2,1,0:T(8,128)(2,1)} %cholesky.1), custom_call_target="tpu_custom_call" | custom-call | tf_op jit(solution)/shard_map/pallas_call | solution.py:454
  70.7 1.7 %shard_map.69 = (f32[2,64,512]{2,1,0:T(8,128)}, f32[2]{0:T(128)}) custom-call(f32[2,64,512]{2,1,0:T(8,128)} %get-tuple-element.4.result, f32[2]{0:T(128)} %get-tuple-element.5.log), custom_call_target="tpu_custom_call" | custom-call | tf_op jit(solution)/shard_map/pallas_call | solution.py:468

commit v6 on v5

--- a/solution.py
+++ b/solution.py
@@ -129,13 +129,13 @@
             send(src, recv_a.at[k, :, chip], pair_sems(k), pos)
         recv_a[k, :, chip] = send_a[k, y * 2 + zh]
 
-    for g in range(STAGES):
-        load(jnp.int32(g))
     wait(walkers, in_sem.at[0])
     wait(inverse, in_sem.at[1])
     rotate(0)
     pl.semaphore_wait(barrier, 64)
     give_rotated(0)
+    for g in range(STAGES):
+        load(jnp.int32(g))
     rotate(1)
     give_rotated(1)
 

time: 72.6 us -> 72.6 us (level)
  no operation moved by 1% of the time
where the time goes in v6:
time: 72.6 us; the launch traced here: 72.4 us
  Pallas kernels  71.7 us (99%)
    pallas_call x1, Pallas kernels, per_device(): pl.pallas_call(kernel, out_shape=(jax.ShapeDtypeStruct(walkers.shape, F32...  70 us
    pallas_call x1, Pallas kernels, per_device(): pl.pallas_call(settle, out_shape=(jax.ShapeDtypeStruct(walkers.shape, F32...  1.69 us

profile of v6, /device:TPU:1, one launch (start us, length us, event | category | flops | bytes accessed | tf_op | source)
XLA Modules:
  0.0 72.4 jit_solution(7155575478620679174)
XLA Ops:
  0.6 70.0 %shard_map.68 = (f32[2,64,512]{2,1,0:T(8,128)}, f32[2]{0:T(128)}) custom-call(f32[2,64,512]{2,1,0:T(8,128)} %walkers_in.1, f32[2,64,64]{2,1,0:T(8,128)} %inverse_in.1, bf16[64,64]{1,0:T(8,128)(2,1)} %trial.1, f32[2,4096]{1,0:T(2,128)} %fields.1, bf16[32,64,4096]{2,1,0:T(8,128)(2,1)} %cholesky.1), custom_call_target="tpu_custom_call" | custom-call | tf_op jit(solution)/shard_map/pallas_call | solution.py:454
  70.7 1.7 %shard_map.69 = (f32[2,64,512]{2,1,0:T(8,128)}, f32[2]{0:T(128)}) custom-call(f32[2,64,512]{2,1,0:T(8,128)} %get-tuple-element.4.result, f32[2]{0:T(128)} %get-tuple-element.5.log), custom_call_target="tpu_custom_call" | custom-call | tf_op jit(solution)/shard_map/pallas_call | solution.py:468
